TPU v7x, 32 devices: a whole 2x2x4 slice. The times are simulated.
32 devices in a mesh: row: 8 (over z, x), col: 4 (over y, core).
Axes of the slice: x: 2, y: 2, z: 4, core: 2. Of those that a mesh axis runs over, the one named last changes fastest.
Arguments:
- affinity: bfloat16 [32768, 8192], P('row', 'col'), may hold values from -250 to 250
- seed_values: int32 [16], replicated, may hold values from 0 to 1073741823
- sku_ids: int32 [8192], P('col'), may hold values from 0 to 8191, each once
Outputs:
- range_basis: float32 [16, 32768], P(None, ('row', 'col'))
- range_factor: float32 [16, 16], replicated
All inputs are finite; a program needn't handle non-finite values.
Results may differ from a plain program's by a relative error of at most 0.0046.
Values may be sent and summed in bfloat16 or wider, within the bound.
A program may use at most 64 MiB of HBM per device.

v0:
```python
import math

import jax
import jax.numpy as jnp
from jax import lax
from jax.sharding import PartitionSpec as P

ITERS = 2


mix_first = -2048144789
mix_second = -1028477387
golden = -1640531535
salt_value = 1540483477


def shifted(value, amount):
    return lax.shift_right_logical(value, jnp.full(value.shape, amount, jnp.int32))


def scramble(value):
    value = jnp.bitwise_xor(value, shifted(value, 16))
    value = value * jnp.int32(mix_first)
    value = jnp.bitwise_xor(value, shifted(value, 13))
    value = value * jnp.int32(mix_second)
    return jnp.bitwise_xor(value, shifted(value, 16))


def test_matrix(seed_values, sku_ids, total_columns):
    first = scramble(jnp.bitwise_xor(seed_values[:, None], sku_ids[None, :] * jnp.int32(golden)))
    second = scramble(jnp.bitwise_xor(first, jnp.int32(salt_value)))
    uniform_a = (shifted(first, 9) + 1).astype(jnp.float32) / 8388608.0
    uniform_b = (shifted(second, 9) + 1).astype(jnp.float32) / 8388608.0
    gauss = jnp.sqrt(-2.0 * jnp.log(uniform_a)) * jnp.cos(6.283185307179586 * uniform_b)
    return (gauss / math.sqrt(total_columns)).astype(jnp.bfloat16)


def lower_solve(lower, right):
    return lax.linalg.triangular_solve(lower, right, left_side=True, lower=True)


def body(affinity, seed_values, sku_ids):
    col_count = lax.axis_size("col")
    total_columns = sku_ids.shape[0] * col_count
    local_rows = affinity.shape[0]
    piece_rows = local_rows // col_count
    total_rows = local_rows * lax.axis_size("row")
    inv_root = 1.0 / math.sqrt(total_columns)

    def project(left):
        return lax.dot_general(
            left, affinity, (((1,), (1,)), ((), ())), preferred_element_type=jnp.float32
        )

    omega = test_matrix(seed_values, sku_ids, total_columns)
    partial_sketch = project(omega)
    for repeat in range(ITERS + 1):
        sketch = lax.psum(partial_sketch, "col")
        gram = lax.psum(
            jnp.dot(
                sketch,
                sketch.T,
                precision=lax.Precision.HIGHEST,
                preferred_element_type=jnp.float32,
            ),
            "row",
        )
        lower = jnp.linalg.cholesky(gram)
        ortho = lower_solve(lower, sketch)
        if repeat < ITERS:
            back_part = jnp.dot(
                ortho.astype(jnp.bfloat16), affinity, preferred_element_type=jnp.float32
            )
        else:
            start_row = lax.axis_index("col") * piece_rows
            ortho = lax.dynamic_slice_in_dim(ortho, start_row, piece_rows, 1)
        if repeat < ITERS:
            back = lax.psum(back_part, "row")
            partial_sketch = project(back.astype(jnp.bfloat16)) * inv_root
    scale = math.sqrt(total_rows)
    return (ortho * scale, lower.T / scale)


def solution(mesh):
    placed = (P("row", "col"), P(), P("col"))
    return jax.shard_map(
        body, mesh=mesh, in_specs=placed, out_specs=(P(None, ("row", "col")), P()), check_vma=False
    )
```

profile of v0, /device:TPU:0, one launch (start us, length us, event | category | flops | bytes accessed | tf_op | source)
XLA Modules:
  0.0 315.6 jit_solution(10747152659197352157)
XLA Ops:
  7.9 11.5 %fusion.12 = f32[16,4096]{1,0:T(8,128)} fusion(bf16[4096,2048]{1,0:T(8,128)(2,1)} %param.6, s32[2048]{0:T(1024)S(1)} %broadcast_multiply_fusion, s32[16]{0:T(128)} %param.7), kind=kOutput, calls=%fused_computation.22 | convolution fusion | flops 269418496 | bytes 17047616 | tf_op jit(solution)/shard_map/dot_general | solution.py:51
  19.5 35.1 %all-reduce.6.cloned.1.call-done = f32[16,4096]{1,0:T(8,128)} async-done(((f32[16,4096]{1,0:T(8,128)}), f32[16,4096]{1,0:T(8,128)}) %all-reduce.6.cloned.1.call-update) | async-done | bytes 262160 | tf_op jit(solution)/shard_map/psum | solution.py:58
  54.6 1.5 fusion.54
  56.1 21.6 %psum.57 = f32[16,16]{0,1:T(8,128)S(1)} all-reduce(f32[16,16]{0,1:T(8,128)S(1)} %fusion.54), channel_id=1, replica_groups=mesh['row'=8,'col'=4] {'row'}, use_global_device_ids=true, to_apply=%region_1.0 | all-reduce | flops 256 | bytes 2048 | tf_op jit(solution)/shard_map/psum | solution.py:59
  77.8 1.5 cholesky.59
  80.6 1.2 custom-call.7
  81.8 1.4 convolution_convert_fusion.1
  83.2 8.0 %fusion.55 = f32[16,2048]{1,0:T(8,128)S(1)} fusion(bf16[16,4096]{1,0:T(8,128)(2,1)S(1)} %convolution_convert_fusion.1, bf16[4096,2048]{1,0:T(8,128)(2,1)} %param.6), kind=kOutput, calls=%fused_computation.79 | convolution fusion | flops 268435456 | bytes 17039360 | tf_op jit(solution)/shard_map/dot_general | solution.py:71
  91.3 34.2 %all-reduce.11 = bf16[16,2048]{1,0:T(8,128)(2,1)S(1)} all-reduce(f32[16,2048]{1,0:T(8,128)S(1)} %fusion.55), channel_id=1, replica_groups=mesh['row'=8,'col'=4] {'row'}, use_global_device_ids=true, to_apply=%region_4.7 | all-reduce | flops 32768 | bytes 196608 | tf_op jit(solution)/shard_map/psum | solution.py:78
  125.5 10.9 %convolution_multiply_fusion.1 = f32[16,4096]{1,0:T(8,128)} fusion(bf16[4096,2048]{1,0:T(8,128)(2,1)} %param.6, bf16[16,2048]{1,0:T(8,128)(2,1)S(1)} %all-reduce.11), kind=kOutput, calls=%fused_computation.1 | convolution fusion | flops 268500992 | bytes 17104896 | tf_op jit(solution)/shard_map/dot_general | solution.py:51
  136.5 30.3 %all-reduce.8.cloned.1.call-done = f32[16,4096]{1,0:T(8,128)} async-done(((f32[16,4096]{1,0:T(8,128)}), f32[16,4096]{1,0:T(8,128)}) %all-reduce.8.cloned.1.call-update) | async-done | bytes 262160 | tf_op jit(solution)/shard_map/psum | solution.py:58
  166.8 1.5 fusion.56
  168.3 21.8 %psum.60 = f32[16,16]{0,1:T(8,128)S(1)} all-reduce(f32[16,16]{0,1:T(8,128)S(1)} %fusion.56), channel_id=1, replica_groups=mesh['row'=8,'col'=4] {'row'}, use_global_device_ids=true, to_apply=%region_6.9 | all-reduce | flops 256 | bytes 2048 | tf_op jit(solution)/shard_map/psum | solution.py:59
  190.2 1.5 cholesky.70
  192.9 1.2 custom-call.8
  194.2 1.4 convolution_convert_fusion
  195.6 8.0 %fusion.57 = f32[16,2048]{1,0:T(8,128)S(1)} fusion(bf16[16,4096]{1,0:T(8,128)(2,1)S(1)} %convolution_convert_fusion, bf16[4096,2048]{1,0:T(8,128)(2,1)} %param.6), kind=kOutput, calls=%fused_computation.81 | convolution fusion | flops 268435456 | bytes 17039360 | tf_op jit(solution)/shard_map/dot_general | solution.py:71
  203.6 34.2 %all-reduce.12 = bf16[16,2048]{1,0:T(8,128)(2,1)S(1)} all-reduce(f32[16,2048]{1,0:T(8,128)S(1)} %fusion.57), channel_id=1, replica_groups=mesh['row'=8,'col'=4] {'row'}, use_global_device_ids=true, to_apply=%region_7.10 | all-reduce | flops 32768 | bytes 196608 | tf_op jit(solution)/shard_map/psum | solution.py:78
  237.8 10.9 %convolution_multiply_fusion = f32[16,4096]{1,0:T(8,128)} fusion(bf16[4096,2048]{1,0:T(8,128)(2,1)} %param.6, bf16[16,2048]{1,0:T(8,128)(2,1)S(1)} %all-reduce.12), kind=kOutput, calls=%fused_computation | convolution fusion | flops 268500992 | bytes 17104896 | tf_op jit(solution)/shard_map/dot_general | solution.py:51
  248.8 30.4 %all-reduce.10.cloned.1.call-done = f32[16,4096]{1,0:T(8,128)} async-done(((f32[16,4096]{1,0:T(8,128)}), f32[16,4096]{1,0:T(8,128)}) %all-reduce.10.cloned.1.call-update) | async-done | bytes 262160 | tf_op jit(solution)/shard_map/psum | solution.py:58
  279.2 1.5 fusion.58
  280.6 21.6 %psum.63 = f32[16,16]{0,1:T(8,128)S(1)} all-reduce(f32[16,16]{0,1:T(8,128)S(1)} %fusion.58), channel_id=1, replica_groups=mesh['row'=8,'col'=4] {'row'}, use_global_device_ids=true, to_apply=%region_9.12 | all-reduce | flops 256 | bytes 2048 | tf_op jit(solution)/shard_map/psum | solution.py:59
  302.3 1.5 cholesky.81
  307.0 1.4 fusion.31
  (25 shorter events, 7.6 us)
Async XLA Ops:
  7.2 47.5 %all-reduce.6.cloned.1.call-start = ((), (), s32[]{:S(2)}) async-start(), calls=%async_computation | async-start | bytes 524288 | tf_op jit(solution)/shard_map/psum | solution.py:58
  19.5 147.3 %all-reduce.8.cloned.1.call-start = ((), (), s32[]{:S(2)}) async-start(), calls=%async_computation.1 | async-start | bytes 524288 | tf_op jit(solution)/shard_map/psum | solution.py:58
  136.4 142.8 %all-reduce.10.cloned.1.call-start = ((), (), s32[]{:S(2)}) async-start(), calls=%async_computation.2 | async-start | bytes 524288 | tf_op jit(solution)/shard_map/psum | solution.py:58
Sparse Core Ops, SparseCore 0:
  19.6 34.9 all-reduce.5
  136.5 30.2 all-reduce.7
  248.9 30.2 all-reduce.9
where the time goes:
time: 316 us
  blocking collectives  133 us (42%)
  waiting for transfers between devices  95.9 us (30%)
  matrix products  58 us (18%)
  between operations  13.8 us (4%)
  other arithmetic  13.4 us (4%)
    psum x3, waiting for transfers between devices, body(): sketch = lax.psum(partial_sketch, 'col')  95.9 us
    psum x2, blocking collectives, body(): back = lax.psum(back_part, 'row')  68.4 us
    psum x3, blocking collectives, body(): lax.psum(jnp.dot(sketch, sketch.T, precision=lax.Precision.HIGHEST, prefe...  65 us
    dot_general x3, matrix products, project(): lax.dot_general(left, affinity, (((1,), (1,)), ((), ())), preferred_eleme...  33.4 us
    dot_general x2, matrix products, body(): jnp.dot(ortho.astype(jnp.bfloat16), affinity, preferred_element_type=jnp....  16.1 us
    another operation x9, other arithmetic, body(): lower = jnp.linalg.cholesky(gram)  6.39 us
  transfers between devices with their start and end apart: 3, of which 3 were waited for; matrix products, arithmetic and copies ran while one was open for 0% of the time, Pallas kernels for 0%

commit v1 on v0

v1 whole, which is shorter than its diff:
```python
import functools
import math

import jax
import jax.numpy as jnp
from jax import lax
from jax.experimental import pallas as pl
from jax.experimental.pallas import tpu as pltpu
from jax.sharding import PartitionSpec as P

ITERS = 2
HIGHEST = lax.Precision.HIGHEST
MESH = pl.DeviceIdType.MESH

mix_first = -2048144789
mix_second = -1028477387
golden = -1640531535
salt_value = 1540483477


def shifted(value, amount):
    return lax.shift_right_logical(value, jnp.full(value.shape, amount, jnp.int32))


def scramble(value):
    value = jnp.bitwise_xor(value, shifted(value, 16))
    value = value * jnp.int32(mix_first)
    value = jnp.bitwise_xor(value, shifted(value, 13))
    value = value * jnp.int32(mix_second)
    return jnp.bitwise_xor(value, shifted(value, 16))


def test_matrix(seeds, skus, total_columns):
    first = scramble(jnp.bitwise_xor(seeds, skus * jnp.int32(golden)))
    second = scramble(jnp.bitwise_xor(first, jnp.int32(salt_value)))
    uniform_a = (shifted(first, 9) + 1).astype(jnp.float32) / 8388608.0
    uniform_b = (shifted(second, 9) + 1).astype(jnp.float32) / 8388608.0
    gauss = jnp.sqrt(-2.0 * jnp.log(uniform_a)) * jnp.cos(6.283185307179586 * uniform_b)
    return (gauss / math.sqrt(total_columns)).astype(jnp.bfloat16)


def factorize(gram):
    count = gram.shape[0]
    rows = lax.broadcasted_iota(jnp.int32, (count, count), 0)
    cols = lax.broadcasted_iota(jnp.int32, (count, count), 1)
    left = gram
    right = (rows == cols).astype(jnp.float32)
    for j in range(count):
        pivot = left[j : j + 1, j : j + 1]
        inv = lax.rsqrt(pivot)
        inv = inv * (1.5 - 0.5 * (pivot * inv) * inv)
        left_row = left[j : j + 1, :] * inv
        right_row = right[j : j + 1, :] * inv
        factor = left[:, j : j + 1] * inv
        left = jnp.where(rows == j, left_row, jnp.where(rows > j, left - factor * left_row, left))
        right = jnp.where(rows == j, right_row, jnp.where(rows > j, right - factor * right_row, right))
    return jnp.where(rows <= cols, left, 0.0), right


def kernel(
    dims,
    slab_hbm, seed_ref, sku_ref,
    basis_ref, factor_ref,
    slab, x_ref, part, sum_recv, s_ref, lhs, zacc, zpart, zrecv, back, gsend_row, grecv_row, grecv_col, gcol,
    load_sem, sum_send_sem, sum_recv_sem, s_send_sem, s_recv_sem,
    z_send_sem, z_recv_sem, b_send_sem, b_recv_sem, g_send_sem, g_recv_sem, c_send_sem, c_recv_sem,
):
    R, C, K, piece, width, inv_root, scale = dims
    w = width // R
    me_r = lax.axis_index("row")
    me_c = lax.axis_index("col")

    def col_peer(k):
        return lax.rem(me_c + k, C)

    def row_peer(k):
        return lax.rem(me_r + k, R)

    def col_from(k):
        return lax.rem(me_c + (C - k), C)

    def row_from(k):
        return lax.rem(me_r + (R - k), R)

    order = list(range(1, C)) + [0]

    def load(k):
        c = col_peer(k)
        return pltpu.make_async_copy(
            slab_hbm.at[pl.ds(pl.multiple_of(c * piece, piece), piece), :], slab.at[c], load_sem.at[k]
        )

    for k in order:
        load(k).start()

    barrier = pltpu.get_barrier_semaphore()
    for k in range(1, R):
        pl.semaphore_signal(barrier, inc=1, device_id={"row": row_peer(k)}, device_id_type=MESH)
    for k in range(1, C):
        pl.semaphore_signal(barrier, inc=1, device_id={"col": col_peer(k)}, device_id_type=MESH)

    index = lax.broadcasted_iota(jnp.int32, (K, width), 0)
    seeds = jnp.zeros((K, width), jnp.int32)
    for k in range(K):
        seeds = jnp.where(index == k, seed_ref[k], seeds)
    x_ref[...] = test_matrix(seeds, jnp.broadcast_to(sku_ref[...], (K, width)), width * C)

    pl.semaphore_wait(barrier, (R - 1) + (C - 1))

    pending = []

    def col_copy(src, dst, send, recv, k):
        return pltpu.make_async_remote_copy(
            src_ref=src, dst_ref=dst, send_sem=send, recv_sem=recv,
            device_id={"col": col_peer(k)}, device_id_type=MESH,
        )

    def row_copy(src, dst, send, recv, k):
        return pltpu.make_async_remote_copy(
            src_ref=src, dst_ref=dst, send_sem=send, recv_sem=recv,
            device_id={"row": row_peer(k)}, device_id_type=MESH,
        )

    def project(c):
        return lax.dot_general(
            x_ref[...], slab[c], (((1,), (1,)), ((), ())), preferred_element_type=jnp.float32
        )

    for it in range(ITERS + 1):
        copies = []
        for k in order:
            if it == 0:
                load(k).wait()
            c = col_peer(k)
            if k == 0:
                own = project(c)
            else:
                part[it, k] = project(c)
                copy = col_copy(
                    part.at[it, k], sum_recv.at[it, k], sum_send_sem.at[it, k], sum_recv_sem.at[it, k], k
                )
                copy.start()
                copies.append((k, copy))
        for k, copy in copies:
            copy.wait_recv()
            own = own + sum_recv[it, k]
            pending.append(copy)
        if it > 0:
            own = own * inv_root

        if it == ITERS:
            gram = lax.dot_general(
                own, own, (((1,), (1,)), ((), ())), precision=HIGHEST, preferred_element_type=jnp.float32
            )
            gcol[...] = gram
            copies = []
            for k in range(1, C):
                copy = col_copy(gcol, grecv_col.at[me_c], c_send_sem.at[k], c_recv_sem.at[k], k)
                copy.start()
                copies.append(copy)
            grecv_col[me_c] = gram
            for k in range(1, C):
                col_copy(
                    gcol, grecv_col.at[col_from(k)], c_send_sem.at[k], c_recv_sem.at[k], k
                ).wait_recv()
            pending += copies
            gram = grecv_col[0]
            for c in range(1, C):
                gram = gram + grecv_col[c]
        else:
            s_ref[it, me_c] = own
            for k in range(1, C):
                copy = col_copy(
                    s_ref.at[it, me_c], s_ref.at[it, me_c], s_send_sem.at[it, k], s_recv_sem.at[it, k], k
                )
                copy.start()
                pending.append(copy)
            gram = None
            for k in range(C):
                c = col_from(k)
                if k > 0:
                    col_copy(
                        s_ref.at[it, c], s_ref.at[it, c], s_send_sem.at[it, k], s_recv_sem.at[it, k], k
                    ).wait_recv()
                value = s_ref[it, c]
                high = value.astype(jnp.bfloat16)
                low = (value - high.astype(jnp.float32)).astype(jnp.bfloat16)
                lhs[:K, :] = high
                lhs[K:, :] = low
                if k < C - 1 or w % 128:
                    product = jnp.dot(lhs[...], slab[c], preferred_element_type=jnp.float32)
                    product = product[:K] + product[K:]
                    zacc[...] = product if k == 0 else zacc[...] + product
            for c in range(C):
                value = s_ref[it, c]
                term = lax.dot_general(
                    value, value, (((1,), (1,)), ((), ())), precision=HIGHEST, preferred_element_type=jnp.float32
                )
                gram = term if c == 0 else gram + term

        gsend_row[it] = gram
        for k in range(1, R):
            copy = row_copy(
                gsend_row.at[it], grecv_row.at[it, me_r], g_send_sem.at[it, k], g_recv_sem.at[it, k], k
            )
            copy.start()
            pending.append(copy)
        grecv_row[it, me_r] = gram

        if it < ITERS:
            last = col_from(C - 1)
            if w % 128:
                for r in range(R):
                    zpart[it, r] = zacc[:, r * w : (r + 1) * w]
            z_copies = []
            for k in list(range(1, R)) + [0]:
                r = row_peer(k)
                if w % 128 == 0:
                    span = pl.ds(pl.multiple_of(r * w, w), w)
                    product = jnp.dot(lhs[...], slab[last, :, span], preferred_element_type=jnp.float32)
                    zpart[it, r] = zacc[:, span] + product[:K] + product[K:]
                if k > 0:
                    copy = row_copy(
                        zpart.at[it, r], zrecv.at[it, k], z_send_sem.at[it, k], z_recv_sem.at[it, k], k
                    )
                    copy.start()
                    z_copies.append((k, copy))

        for k in range(1, R):
            row_copy(
                gsend_row.at[it], grecv_row.at[it, row_from(k)], g_send_sem.at[it, k], g_recv_sem.at[it, k], k
            ).wait_recv()
        gram = grecv_row[it, 0]
        for r in range(1, R):
            gram = gram + grecv_row[it, r]
        upper, inverse = factorize(gram)

        if it == ITERS:
            ortho = jnp.dot(inverse, own, precision=HIGHEST, preferred_element_type=jnp.float32)
            basis_ref[...] = ortho * scale
            factor_ref[...] = upper / scale
        else:
            total = zpart[it, me_r]
            for k, copy in z_copies:
                copy.wait_recv()
                total = total + zrecv[it, k]
                pending.append(copy)
            back[it, me_r] = jnp.dot(
                inverse, total, precision=HIGHEST, preferred_element_type=jnp.float32
            ).astype(jnp.bfloat16)
            for k in range(1, R):
                copy = row_copy(
                    back.at[it, me_r], back.at[it, me_r], b_send_sem.at[it, k], b_recv_sem.at[it, k], k
                )
                copy.start()
                pending.append(copy)
            for k in range(1, R):
                r = row_from(k)
                row_copy(
                    back.at[it, r], back.at[it, r], b_send_sem.at[it, k], b_recv_sem.at[it, k], k
                ).wait_recv()
            for r in range(R):
                x_ref[:, r * w : (r + 1) * w] = back[it, r]

    for copy in pending:
        copy.wait_send()


def body(affinity, seed_values, sku_ids):
    R, C = lax.axis_size("row"), lax.axis_size("col")
    K = seed_values.shape[0]
    rows, width = affinity.shape
    piece, w = rows // C, width // R
    dims = (R, C, K, piece, width, 1.0 / math.sqrt(width * C), math.sqrt(rows * R))
    f32, bf16 = jnp.float32, jnp.bfloat16
    dma = pltpu.SemaphoreType.DMA
    vmem = pl.BlockSpec(memory_space=pltpu.VMEM)
    return pl.pallas_call(
        functools.partial(kernel, dims),
        out_shape=(
            jax.ShapeDtypeStruct((K, piece), f32),
            jax.ShapeDtypeStruct((K, K), f32),
        ),
        in_specs=[
            pl.BlockSpec(memory_space=pl.ANY),
            pl.BlockSpec(memory_space=pltpu.SMEM),
            vmem,
        ],
        out_specs=(vmem, vmem),
        scratch_shapes=[
            pltpu.VMEM((C, piece, width), bf16),
            pltpu.VMEM((K, width), bf16),
            pltpu.VMEM((ITERS + 1, C, K, piece), f32),
            pltpu.VMEM((ITERS + 1, C, K, piece), f32),
            pltpu.VMEM((ITERS, C, K, piece), f32),
            pltpu.VMEM((2 * K, piece), bf16),
            pltpu.VMEM((K, width), f32),
            pltpu.VMEM((ITERS, R, K, w), f32),
            pltpu.VMEM((ITERS, R, K, w), f32),
            pltpu.VMEM((ITERS, R, K, w), bf16),
            pltpu.VMEM((ITERS + 1, K, K), f32),
            pltpu.VMEM((ITERS + 1, R, K, K), f32),
            pltpu.VMEM((C, K, K), f32),
            pltpu.VMEM((K, K), f32),
            dma((C,)),
            dma((ITERS + 1, C)), dma((ITERS + 1, C)),
            dma((ITERS, C)), dma((ITERS, C)),
            dma((ITERS, R)), dma((ITERS, R)),
            dma((ITERS, R)), dma((ITERS, R)),
            dma((ITERS + 1, R)), dma((ITERS + 1, R)),
            dma((C,)), dma((C,)),
        ],
        compiler_params=pltpu.CompilerParams(
            collective_id=0, has_side_effects=True, vmem_limit_bytes=60 * 1024 * 1024
        ),
    )(affinity, seed_values, sku_ids[None, :])


def solution(mesh):
    placed = (P("row", "col"), P(), P("col"))
    return jax.shard_map(
        body, mesh=mesh, in_specs=placed, out_specs=(P(None, ("row", "col")), P()), check_vma=False
    )
```

time: 316 us -> 73.3 us (0.23)
  blocking collectives: 133 us -> 0 us
  waiting for transfers between devices: 95.9 us -> 0 us
  Pallas kernels: 0 us -> 69.7 us
  matrix products: 58 us -> 0 us
  other arithmetic: 13.4 us -> 0 us
  between operations: 13.8 us -> 0.64 us
    psum x5 -> x0, blocking collectives: 133 us -> none  [the longest x2 68.4 us: body(): back = lax.psum(back_part, 'row')]
    psum x3 -> x0, waiting for transfers between devices: 95.9 us -> none  [body(): sketch = lax.psum(partial_sketch, 'col')]
    pallas_call x0 -> x1, Pallas kernels: none -> 69.7 us  [body(): pl.pallas_call(functools.partial(kernel, dims), out_shape=(jax.ShapeDtype...]
    dot_general x8 -> x0, matrix products: 53.9 us -> none  [the longest x3 33.4 us: project(): lax.dot_general(left, affinity, (((1,), (1,)), ((), ())), preferred_eleme...]
    another operation x14 -> x0, other arithmetic: 11.4 us -> none  [the longest x9 6.39 us: body(): lower = jnp.linalg.cholesky(gram)]
    another operation x3 -> x0, matrix products: 4.11 us -> none  [lower_solve(): return lax.linalg.triangular_solve(lower, right, left_side=True, lower=True)]
  transfers between devices with their start and end apart: 3 -> 0, of which waited for: 3 -> 0; matrix products, arithmetic and copies ran while one was open for 0% -> 0% of each run, Pallas kernels for 0% -> 0%
where the time goes in v1:
time: 73.3 us; the launch traced here: 73.1 us
  Pallas kernels  69.7 us (95%)
  local copies, waits for them, and re-layouts  2.77 us (4%)
    pallas_call x1, Pallas kernels, body(): pl.pallas_call(functools.partial(kernel, dims), out_shape=(jax.ShapeDtype...  69.7 us
    unnamed x2, local copies, waits for them, and re-layouts  2.77 us

profile of v1, /device:TPU:0, one launch (start us, length us, event | category | flops | bytes accessed | tf_op | source)
XLA Modules:
  0.0 73.1 jit_solution(13153019037716232989)
XLA Ops:
  0.6 69.7 %shard_map.50 = (f32[16,1024]{1,0:T(8,128)}, f32[16,16]{1,0:T(8,128)}) custom-call(bf16[4096,2048]{1,0:T(8,128)(2,1)} %slab_hbm.1, s32[16]{0:T(128)} %seed_ref.1, s32[1,2048]{1,0:T(1,128)} %bitcast.1), custom_call_target="tpu_custom_call" | custom-call | tf_op jit(solution)/shard_map/pallas_call | solution.py:278
  70.3 1.5 %copy.7 = f32[16,1024]{1,0:T(8,128)} copy(f32[16,1024]{1,0:T(8,128)} %get-tuple-element.4) | data formatting | bytes 131072
  71.8 1.3 %copy.8 = f32[16,16]{1,0:T(8,128)} copy(f32[16,16]{1,0:T(8,128)} %get-tuple-element.5) | data formatting | bytes 2048

commit v2 on v1

--- a/solution.py
+++ b/solution.py
@@ -61,8 +61,9 @@
     dims,
     slab_hbm, seed_ref, sku_ref,
     basis_ref, factor_ref,
-    slab, x_ref, part, sum_recv, s_ref, lhs, zacc, zpart, zrecv, back, gsend_row, grecv_row, grecv_col, gcol,
-    load_sem, sum_send_sem, sum_recv_sem, s_send_sem, s_recv_sem,
+    slab, slab_t, x_ref, part, half_recv, y_sum, part_last, recv_last, s_ref, lhs, zacc, zpart, zrecv, back,
+    gsend_row, grecv_row, grecv_col, gcol, gram_part,
+    load_sem, a_send_sem, a_recv_sem, y_send_sem, y_recv_sem, last_send_sem, last_recv_sem, s_send_sem, s_recv_sem,
     z_send_sem, z_recv_sem, b_send_sem, b_recv_sem, g_send_sem, g_recv_sem, c_send_sem, c_recv_sem,
 ):
     R, C, K, piece, width, inv_root, scale = dims
@@ -70,34 +71,36 @@
     me_r = lax.axis_index("row")
     me_c = lax.axis_index("col")
 
-    def col_peer(k):
-        return lax.rem(me_c + k, C)
+    Y = C // 2
+    core, me_y = lax.rem(me_c, 2), me_c // 2
+    partner = me_y * 2 + (1 - core)
+
+    def y_peer(k):
+        return lax.rem(me_y + k, Y) * 2 + core
+
+    def col_peer_of(k):
+        return (1 - core) * Y + k if k < Y else core * Y + k - Y
 
     def row_peer(k):
         return lax.rem(me_r + k, R)
 
-    def col_from(k):
-        return lax.rem(me_c + (C - k), C)
-
     def row_from(k):
         return lax.rem(me_r + (R - k), R)
 
-    order = list(range(1, C)) + [0]
-
     def load(k):
-        c = col_peer(k)
+        c = col_peer_of(k)
         return pltpu.make_async_copy(
             slab_hbm.at[pl.ds(pl.multiple_of(c * piece, piece), piece), :], slab.at[c], load_sem.at[k]
         )
 
-    for k in order:
+    for k in range(C):
         load(k).start()
 
     barrier = pltpu.get_barrier_semaphore()
     for k in range(1, R):
         pl.semaphore_signal(barrier, inc=1, device_id={"row": row_peer(k)}, device_id_type=MESH)
     for k in range(1, C):
-        pl.semaphore_signal(barrier, inc=1, device_id={"col": col_peer(k)}, device_id_type=MESH)
+        pl.semaphore_signal(barrier, inc=1, device_id={"col": lax.rem(me_c + k, C)}, device_id_type=MESH)
 
     index = lax.broadcasted_iota(jnp.int32, (K, width), 0)
     seeds = jnp.zeros((K, width), jnp.int32)
@@ -109,10 +112,10 @@
 
     pending = []
 
-    def col_copy(src, dst, send, recv, k):
+    def col_copy(src, dst, send, recv, target):
         return pltpu.make_async_remote_copy(
             src_ref=src, dst_ref=dst, send_sem=send, recv_sem=recv,
-            device_id={"col": col_peer(k)}, device_id_type=MESH,
+            device_id={"col": lax.rem(target, C)}, device_id_type=MESH,
         )
 
     def row_copy(src, dst, send, recv, k):
@@ -122,81 +125,118 @@
         )
 
     def project(c):
+        return jnp.dot(x_ref[...], slab_t[c], preferred_element_type=jnp.float32)
+
+    def fetch(k):
+        load(k).wait()
+        c = col_peer_of(k)
+        slab_t[c] = slab[c].T
+
+    def square(value):
         return lax.dot_general(
-            x_ref[...], slab[c], (((1,), (1,)), ((), ())), preferred_element_type=jnp.float32
+            value, value, (((1,), (1,)), ((), ())), precision=HIGHEST, preferred_element_type=jnp.float32
         )
 
     for it in range(ITERS + 1):
-        copies = []
-        for k in order:
-            if it == 0:
-                load(k).wait()
-            c = col_peer(k)
-            if k == 0:
-                own = project(c)
-            else:
-                part[it, k] = project(c)
-                copy = col_copy(
-                    part.at[it, k], sum_recv.at[it, k], sum_send_sem.at[it, k], sum_recv_sem.at[it, k], k
-                )
-                copy.start()
-                copies.append((k, copy))
-        for k, copy in copies:
-            copy.wait_recv()
-            own = own + sum_recv[it, k]
-            pending.append(copy)
-        if it > 0:
+        if it == ITERS:
+            copies = []
+            for k in list(range(1, C)) + [0]:
+                c = lax.rem(me_c + k, C)
+                if k == 0:
+                    own = project(c)
+                else:
+                    part_last[k] = project(c)
+                    copy = col_copy(
+                        part_last.at[k], recv_last.at[k], last_send_sem.at[k], last_recv_sem.at[k], me_c + k
+                    )
+                    copy.start()
+                    copies.append(copy)
+            for k, copy in enumerate(copies):
+                copy.wait_recv()
+                own = own + recv_last[k + 1]
+            pending += copies
             own = own * inv_root
-
-        if it == ITERS:
-            gram = lax.dot_general(
-                own, own, (((1,), (1,)), ((), ())), precision=HIGHEST, preferred_element_type=jnp.float32
-            )
+            gram = square(own)
             gcol[...] = gram
             copies = []
             for k in range(1, C):
-                copy = col_copy(gcol, grecv_col.at[me_c], c_send_sem.at[k], c_recv_sem.at[k], k)
+                copy = col_copy(gcol, grecv_col.at[me_c], c_send_sem.at[k], c_recv_sem.at[k], me_c + k)
                 copy.start()
                 copies.append(copy)
             grecv_col[me_c] = gram
             for k in range(1, C):
+                source = lax.rem(me_c + (C - k), C)
                 col_copy(
-                    gcol, grecv_col.at[col_from(k)], c_send_sem.at[k], c_recv_sem.at[k], k
+                    gcol, grecv_col.at[source], c_send_sem.at[k], c_recv_sem.at[k], me_c + k
                 ).wait_recv()
             pending += copies
             gram = grecv_col[0]
             for c in range(1, C):
                 gram = gram + grecv_col[c]
         else:
-            s_ref[it, me_c] = own
-            for k in range(1, C):
+            for q in range(Y):
+                if it == 0:
+                    fetch(q)
+                part[it, q] = project((1 - core) * Y + q)
                 copy = col_copy(
-                    s_ref.at[it, me_c], s_ref.at[it, me_c], s_send_sem.at[it, k], s_recv_sem.at[it, k], k
+                    part.at[it, q], half_recv.at[it, q], a_send_sem.at[it, q], a_recv_sem.at[it, q], partner
                 )
                 copy.start()
                 pending.append(copy)
+            for q in range(Y):
+                if it == 0:
+                    fetch(Y + q)
+                value = project(core * Y + q)
+                col_copy(
+                    part.at[it, q], half_recv.at[it, q], a_send_sem.at[it, q], a_recv_sem.at[it, q], partner
+                ).wait_recv()
+                y_sum[it, q, me_y] = value + half_recv[it, q]
+                for k in range(1, Y):
+                    copy = col_copy(
+                        y_sum.at[it, q, me_y], y_sum.at[it, q, me_y],
+                        y_send_sem.at[it, q, k], y_recv_sem.at[it, q, k], y_peer(k),
+                    )
+                    copy.start()
+                    pending.append(copy)
             gram = None
-            for k in range(C):
-                c = col_from(k)
-                if k > 0:
+            for q in range(C):
+                if q < Y:
+                    c = core * Y + q
+                    for k in range(1, Y):
+                        source = lax.rem(me_y + (Y - k), Y)
+                        col_copy(
+                            y_sum.at[it, q, source], y_sum.at[it, q, source],
+                            y_send_sem.at[it, q, k], y_recv_sem.at[it, q, k], y_peer(k),
+                        ).wait_recv()
+                    value = y_sum[it, q, 0]
+                    for y in range(1, Y):
+                        value = value + y_sum[it, q, y]
+                    if it > 0:
+                        value = value * inv_root
+                    s_ref[it, c] = value
+                    copy = col_copy(
+                        s_ref.at[it, c], s_ref.at[it, c], s_send_sem.at[it, q], s_recv_sem.at[it, q], partner
+                    )
+                    copy.start()
+                    pending.append(copy)
+                else:
+                    c = (1 - core) * Y + q - Y
                     col_copy(
-                        s_ref.at[it, c], s_ref.at[it, c], s_send_sem.at[it, k], s_recv_sem.at[it, k], k
+                        s_ref.at[it, c], s_ref.at[it, c], s_send_sem.at[it, q - Y], s_recv_sem.at[it, q - Y], partner
                     ).wait_recv()
-                value = s_ref[it, c]
+                    value = s_ref[it, c]
                 high = value.astype(jnp.bfloat16)
                 low = (value - high.astype(jnp.float32)).astype(jnp.bfloat16)
                 lhs[:K, :] = high
                 lhs[K:, :] = low
-                if k < C - 1 or w % 128:
+                if q < C - 1 or w % 128:
                     product = jnp.dot(lhs[...], slab[c], preferred_element_type=jnp.float32)
                     product = product[:K] + product[K:]
-                    zacc[...] = product if k == 0 else zacc[...] + product
-            for c in range(C):
-                value = s_ref[it, c]
-                term = lax.dot_general(
-                    value, value, (((1,), (1,)), ((), ())), precision=HIGHEST, preferred_element_type=jnp.float32
-                )
-                gram = term if c == 0 else gram + term
+                    zacc[...] = product if q == 0 else zacc[...] + product
+                gram_part[it, c] = square(value)
+            gram = gram_part[it, 0]
+            for c in range(1, C):
+                gram = gram + gram_part[it, c]
 
         gsend_row[it] = gram
         for k in range(1, R):
@@ -208,7 +248,7 @@
         grecv_row[it, me_r] = gram
 
         if it < ITERS:
-            last = col_from(C - 1)
+            last = (1 - core) * Y + Y - 1
             if w % 128:
                 for r in range(R):
                     zpart[it, r] = zacc[:, r * w : (r + 1) * w]
@@ -270,7 +310,7 @@
     R, C = lax.axis_size("row"), lax.axis_size("col")
     K = seed_values.shape[0]
     rows, width = affinity.shape
-    piece, w = rows // C, width // R
+    piece, w, Y = rows // C, width // R, C // 2
     dims = (R, C, K, piece, width, 1.0 / math.sqrt(width * C), math.sqrt(rows * R))
     f32, bf16 = jnp.float32, jnp.bfloat16
     dma = pltpu.SemaphoreType.DMA
@@ -289,9 +329,13 @@
         out_specs=(vmem, vmem),
         scratch_shapes=[
             pltpu.VMEM((C, piece, width), bf16),
+            pltpu.VMEM((C, width, piece), bf16),
             pltpu.VMEM((K, width), bf16),
-            pltpu.VMEM((ITERS + 1, C, K, piece), f32),
-            pltpu.VMEM((ITERS + 1, C, K, piece), f32),
+            pltpu.VMEM((ITERS, Y, K, piece), f32),
+            pltpu.VMEM((ITERS, Y, K, piece), f32),
+            pltpu.VMEM((ITERS, Y, Y, K, piece), f32),
+            pltpu.VMEM((C, K, piece), f32),
+            pltpu.VMEM((C, K, piece), f32),
             pltpu.VMEM((ITERS, C, K, piece), f32),
             pltpu.VMEM((2 * K, piece), bf16),
             pltpu.VMEM((K, width), f32),
@@ -302,9 +346,12 @@
             pltpu.VMEM((ITERS + 1, R, K, K), f32),
             pltpu.VMEM((C, K, K), f32),
             pltpu.VMEM((K, K), f32),
+            pltpu.VMEM((ITERS, C, K, K), f32),
             dma((C,)),
-            dma((ITERS + 1, C)), dma((ITERS + 1, C)),
-            dma((ITERS, C)), dma((ITERS, C)),
+            dma((ITERS, Y)), dma((ITERS, Y)),
+            dma((ITERS, Y, Y)), dma((ITERS, Y, Y)),
+            dma((C,)), dma((C,)),
+            dma((ITERS, Y)), dma((ITERS, Y)),
             dma((ITERS, R)), dma((ITERS, R)),
             dma((ITERS, R)), dma((ITERS, R)),
             dma((ITERS + 1, R)), dma((ITERS + 1, R)),

time: 73.3 us -> 67.9 us (0.926)
  Pallas kernels: 69.7 us -> 64.3 us
    pallas_call x1, Pallas kernels: 69.7 us -> 64.3 us  [body(): pl.pallas_call(functools.partial(kernel, dims), out_shape=(jax.ShapeDtype...]
where the time goes in v2:
time: 67.9 us; the launch traced here: 67.7 us
  Pallas kernels  64.3 us (95%)
  local copies, waits for them, and re-layouts  2.77 us (4%)
    pallas_call x1, Pallas kernels, body(): pl.pallas_call(functools.partial(kernel, dims), out_shape=(jax.ShapeDtype...  64.3 us
    unnamed x2, local copies, waits for them, and re-layouts  2.77 us

profile of v2, /device:TPU:0, one launch (start us, length us, event | category | flops | bytes accessed | tf_op | source)
XLA Modules:
  0.0 67.7 jit_solution(10589236261814951172)
XLA Ops:
  0.6 64.3 %shard_map.50 = (f32[16,1024]{1,0:T(8,128)}, f32[16,16]{1,0:T(8,128)}) custom-call(bf16[4096,2048]{1,0:T(8,128)(2,1)} %slab_hbm.1, s32[16]{0:T(128)} %seed_ref.1, s32[1,2048]{1,0:T(1,128)} %bitcast.1), custom_call_target="tpu_custom_call" | custom-call | tf_op jit(solution)/shard_map/pallas_call | solution.py:318
  64.9 1.5 %copy.7 = f32[16,1024]{1,0:T(8,128)} copy(f32[16,1024]{1,0:T(8,128)} %get-tuple-element.4) | data formatting | bytes 131072
  66.4 1.3 %copy.8 = f32[16,16]{1,0:T(8,128)} copy(f32[16,16]{1,0:T(8,128)} %get-tuple-element.5) | data formatting | bytes 2048

commit v3 on v2

--- a/solution.py
+++ b/solution.py
@@ -9,6 +9,8 @@
 from jax.sharding import PartitionSpec as P
 
 ITERS = 2
+SUB = 2
+DEPTH = 3
 HIGHEST = lax.Precision.HIGHEST
 MESH = pl.DeviceIdType.MESH
 
@@ -62,7 +64,7 @@
     slab_hbm, seed_ref, sku_ref,
     basis_ref, factor_ref,
     slab, slab_t, x_ref, part, half_recv, y_sum, part_last, recv_last, s_ref, lhs, zacc, zpart, zrecv, back,
-    gsend_row, grecv_row, grecv_col, gcol, gram_part,
+    gsend_row, grecv_row, grecv_col, gcol, gram_part, mine,
     load_sem, a_send_sem, a_recv_sem, y_send_sem, y_recv_sem, last_send_sem, last_recv_sem, s_send_sem, s_recv_sem,
     z_send_sem, z_recv_sem, b_send_sem, b_recv_sem, g_send_sem, g_recv_sem, c_send_sem, c_recv_sem,
 ):
@@ -87,14 +89,19 @@
     def row_from(k):
         return lax.rem(me_r + (R - k), R)
 
-    def load(k):
-        c = col_peer_of(k)
+    span = piece // SUB
+    n_load = C * SUB
+
+    def load(i):
+        start = col_peer_of(i // SUB) * piece + (i % SUB) * span
         return pltpu.make_async_copy(
-            slab_hbm.at[pl.ds(pl.multiple_of(c * piece, piece), piece), :], slab.at[c], load_sem.at[k]
-        )
-
-    for k in range(C):
-        load(k).start()
+            slab_hbm.at[pl.ds(pl.multiple_of(start, span), span), :],
+            slab.at[i // SUB, pl.ds((i % SUB) * span, span), :],
+            load_sem.at[i],
+        )
+
+    for i in range(min(DEPTH, n_load)):
+        load(i).start()
 
     barrier = pltpu.get_barrier_semaphore()
     for k in range(1, R):
@@ -124,13 +131,33 @@
             device_id={"row": row_peer(k)}, device_id_type=MESH,
         )
 
-    def project(c):
-        return jnp.dot(x_ref[...], slab_t[c], preferred_element_type=jnp.float32)
-
-    def fetch(k):
-        load(k).wait()
-        c = col_peer_of(k)
-        slab_t[c] = slab[c].T
+    def project(k):
+        return jnp.dot(x_ref[...], slab_t[k], preferred_element_type=jnp.float32)
+
+    def position(c):
+        half = c // Y
+        same = 1 - (half + core - 2 * half * core)
+        return lax.rem(c, Y) + Y * same
+
+    def send_half(it, q):
+        copy = col_copy(
+            part.at[it, q], half_recv.at[it, q], a_send_sem.at[it, q], a_recv_sem.at[it, q], partner
+        )
+        copy.start()
+        pending.append(copy)
+
+    def send_y(it, q, value):
+        col_copy(
+            part.at[it, q], half_recv.at[it, q], a_send_sem.at[it, q], a_recv_sem.at[it, q], partner
+        ).wait_recv()
+        y_sum[it, q, me_y] = value + half_recv[it, q]
+        for k in range(1, Y):
+            copy = col_copy(
+                y_sum.at[it, q, me_y], y_sum.at[it, q, me_y],
+                y_send_sem.at[it, q, k], y_recv_sem.at[it, q, k], y_peer(k),
+            )
+            copy.start()
+            pending.append(copy)
 
     def square(value):
         return lax.dot_general(
@@ -140,20 +167,18 @@
     for it in range(ITERS + 1):
         if it == ITERS:
             copies = []
-            for k in list(range(1, C)) + [0]:
-                c = lax.rem(me_c + k, C)
-                if k == 0:
-                    own = project(c)
-                else:
-                    part_last[k] = project(c)
-                    copy = col_copy(
-                        part_last.at[k], recv_last.at[k], last_send_sem.at[k], last_recv_sem.at[k], me_c + k
-                    )
-                    copy.start()
-                    copies.append(copy)
-            for k, copy in enumerate(copies):
-                copy.wait_recv()
-                own = own + recv_last[k + 1]
+            for k in list(range(2, C)) + [1]:
+                target = lax.rem(me_y + k // 2, Y) * 2 + (1 - core if k % 2 else core)
+                part_last[k] = project(position(target))
+                copy = col_copy(
+                    part_last.at[k], recv_last.at[k], last_send_sem.at[k], last_recv_sem.at[k], target
+                )
+                copy.start()
+                copies.append(copy)
+            own = project(position(me_c))
+            for k in [1] + list(range(2, C)):
+                copies[(k - 2) % (C - 1)].wait_recv()
+                own = own + recv_last[k]
             pending += copies
             own = own * inv_root
             gram = square(own)
@@ -174,32 +199,35 @@
             for c in range(1, C):
                 gram = gram + grecv_col[c]
         else:
-            for q in range(Y):
-                if it == 0:
-                    fetch(q)
-                part[it, q] = project((1 - core) * Y + q)
-                copy = col_copy(
-                    part.at[it, q], half_recv.at[it, q], a_send_sem.at[it, q], a_recv_sem.at[it, q], partner
-                )
-                copy.start()
-                pending.append(copy)
-            for q in range(Y):
-                if it == 0:
-                    fetch(Y + q)
-                value = project(core * Y + q)
-                col_copy(
-                    part.at[it, q], half_recv.at[it, q], a_send_sem.at[it, q], a_recv_sem.at[it, q], partner
-                ).wait_recv()
-                y_sum[it, q, me_y] = value + half_recv[it, q]
-                for k in range(1, Y):
-                    copy = col_copy(
-                        y_sum.at[it, q, me_y], y_sum.at[it, q, me_y],
-                        y_send_sem.at[it, q, k], y_recv_sem.at[it, q, k], y_peer(k),
-                    )
-                    copy.start()
-                    pending.append(copy)
+            if it == 0:
+                for i in range(n_load + 1):
+                    if i < n_load:
+                        load(i).wait()
+                        if i + DEPTH < n_load:
+                            load(i + DEPTH).start()
+                        here = slice((i % SUB) * span, (i % SUB + 1) * span)
+                        slab_t[i // SUB, :, here] = slab[i // SUB, here, :].T
+                    if i > 0:
+                        k, sub = (i - 1) // SUB, (i - 1) % SUB
+                        here = slice(sub * span, (sub + 1) * span)
+                        value = jnp.dot(x_ref[...], slab_t[k, :, here], preferred_element_type=jnp.float32)
+                        if k < Y:
+                            part[it, k, :, here] = value
+                            if sub == SUB - 1:
+                                send_half(it, k)
+                        else:
+                            mine[:, here] = value
+                            if sub == SUB - 1:
+                                send_y(it, k - Y, mine[...])
+            else:
+                for q in range(Y):
+                    part[it, q] = project(q)
+                    send_half(it, q)
+                for q in range(Y):
+                    send_y(it, q, project(Y + q))
             gram = None
             for q in range(C):
+                at = Y + q if q < Y else q - Y
                 if q < Y:
                     c = core * Y + q
                     for k in range(1, Y):
@@ -230,7 +258,7 @@
                 lhs[:K, :] = high
                 lhs[K:, :] = low
                 if q < C - 1 or w % 128:
-                    product = jnp.dot(lhs[...], slab[c], preferred_element_type=jnp.float32)
+                    product = jnp.dot(lhs[...], slab[at], preferred_element_type=jnp.float32)
                     product = product[:K] + product[K:]
                     zacc[...] = product if q == 0 else zacc[...] + product
                 gram_part[it, c] = square(value)
@@ -248,7 +276,7 @@
         grecv_row[it, me_r] = gram
 
         if it < ITERS:
-            last = (1 - core) * Y + Y - 1
+            last = Y - 1
             if w % 128:
                 for r in range(R):
                     zpart[it, r] = zacc[:, r * w : (r + 1) * w]
@@ -256,9 +284,9 @@
             for k in list(range(1, R)) + [0]:
                 r = row_peer(k)
                 if w % 128 == 0:
-                    span = pl.ds(pl.multiple_of(r * w, w), w)
-                    product = jnp.dot(lhs[...], slab[last, :, span], preferred_element_type=jnp.float32)
-                    zpart[it, r] = zacc[:, span] + product[:K] + product[K:]
+                    cols = pl.ds(pl.multiple_of(r * w, w), w)
+                    product = jnp.dot(lhs[...], slab[last, :, cols], preferred_element_type=jnp.float32)
+                    zpart[it, r] = zacc[:, cols] + product[:K] + product[K:]
                 if k > 0:
                     copy = row_copy(
                         zpart.at[it, r], zrecv.at[it, k], z_send_sem.at[it, k], z_recv_sem.at[it, k], k
@@ -347,7 +375,8 @@
             pltpu.VMEM((C, K, K), f32),
             pltpu.VMEM((K, K), f32),
             pltpu.VMEM((ITERS, C, K, K), f32),
-            dma((C,)),
+            pltpu.VMEM((K, piece), f32),
+            dma((C * SUB,)),
             dma((ITERS, Y)), dma((ITERS, Y)),
             dma((ITERS, Y, Y)), dma((ITERS, Y, Y)),
             dma((C,)), dma((C,)),

time: 67.9 us -> 66.6 us (0.981)
  Pallas kernels: 64.3 us -> 62.9 us
    pallas_call x1, Pallas kernels: 64.3 us -> 62.9 us  [body(): pl.pallas_call(functools.partial(kernel, dims), out_shape=(jax.ShapeDtype...]
where the time goes in v3:
time: 66.6 us; the launch traced here: 66.3 us
  Pallas kernels  62.9 us (94%)
  local copies, waits for them, and re-layouts  2.77 us (4%)
    pallas_call x1, Pallas kernels, body(): pl.pallas_call(functools.partial(kernel, dims), out_shape=(jax.ShapeDtype...  62.9 us
    unnamed x2, local copies, waits for them, and re-layouts  2.77 us

profile of v3, /device:TPU:0, one launch (start us, length us, event | category | flops | bytes accessed | tf_op | source)
XLA Modules:
  0.0 66.3 jit_solution(7436596084420236882)
XLA Ops:
  0.6 62.9 %shard_map.50 = (f32[16,1024]{1,0:T(8,128)}, f32[16,16]{1,0:T(8,128)}) custom-call(bf16[4096,2048]{1,0:T(8,128)(2,1)} %slab_hbm.1, s32[16]{0:T(128)} %seed_ref.1, s32[1,2048]{1,0:T(1,128)} %bitcast.1), custom_call_target="tpu_custom_call" | custom-call | tf_op jit(solution)/shard_map/pallas_call | solution.py:346
  63.5 1.5 %copy.7 = f32[16,1024]{1,0:T(8,128)} copy(f32[16,1024]{1,0:T(8,128)} %get-tuple-element.4) | data formatting | bytes 131072
  65.0 1.3 %copy.8 = f32[16,16]{1,0:T(8,128)} copy(f32[16,16]{1,0:T(8,128)} %get-tuple-element.5) | data formatting | bytes 2048
